TPU v7x, 512 devices: a whole 4x8x8 slice. The times are simulated.
512 devices in a mesh: row: 16 (over y, core), col: 32 (over x, z).
Axes of the slice: x: 4, y: 8, z: 8, core: 2. Of those that a mesh axis runs over, the one named last changes fastest.
Arguments:
- outcome_vectors: bfloat16 [16384, 1024], P('row', 'col'), may hold values from -6 to 6
- u_factor: bfloat16 [32, 1024], P(None, 'col'), may hold values from -0.03125 to 0.03125
- v_factor: bfloat16 [32, 1024], P(None, 'col'), may hold values from -0.03125 to 0.03125
- outcome_index: int32 [16384], replicated, may hold values from 0 to 16383, each once
Outputs:
- factored: float32 [16384, 16384], P('row', 'col')
All inputs are finite; a program needn't handle non-finite values.
Results may differ from a plain program's by a relative error of at most 0.0056.
Values may be sent and summed in bfloat16 or wider, within the bound.
A program may use at most 64 MiB of HBM per device.

v0:
```python
import jax
import jax.numpy as jnp
from jax import lax
from jax.sharding import PartitionSpec as P

PANEL = 256
NPANEL = 2


def from_root(block, axis, holder):
    block = jnp.where(lax.axis_index(axis) == holder, block, jnp.zeros_like(block))
    return lax.psum(block, axis)


def body(outcome_vectors, u_factor, v_factor, outcome_index):
    rank = u_factor.shape[0]
    factors = jnp.concatenate([u_factor, v_factor], axis=0)
    partial_value = lax.dot_general(
        factors, outcome_vectors, (((1,), (1,)), ((), ())), preferred_element_type=jnp.float32
    )
    summed = lax.psum(partial_value, "col")
    table = lax.all_gather(summed.astype(jnp.bfloat16), "row", axis=1, tiled=True)
    total = table.shape[1]
    row_height = total // lax.axis_size("row")
    col_width = total // lax.axis_size("col")
    row_start = lax.axis_index("row") * row_height
    col_start = lax.axis_index("col") * col_width
    row_ids = lax.dynamic_slice_in_dim(outcome_index, row_start, row_height)
    col_ids = lax.dynamic_slice_in_dim(outcome_index, col_start, col_width)
    row_vecs = jnp.take(table, row_ids, axis=1)
    col_vecs = jnp.take(table, col_ids, axis=1)
    over_first = (((0,), (0,)), ((), ()))
    over_second = (((1,), (1,)), ((), ()))
    gram_u = lax.dot_general(
        row_vecs[:rank], col_vecs[:rank], over_first, preferred_element_type=jnp.float32
    )
    gram_v = lax.dot_general(
        row_vecs[rank:], col_vecs[rank:], over_first, preferred_element_type=jnp.float32
    )
    rows_global = row_start + jnp.arange(row_height, dtype=jnp.int32)[:, None]
    cols_global = col_start + jnp.arange(col_width, dtype=jnp.int32)[None, :]
    schur = gram_u * gram_v + (rows_global == cols_global).astype(jnp.float32)
    for step in range(NPANEL):
        start = step * PANEL
        stop = start + PANEL
        owner_col = start // col_width
        offset_col = start % col_width
        owner_row = start // row_height
        offset_row = start % row_height
        panel_cols = start + jnp.arange(PANEL, dtype=jnp.int32)[None, :]
        panel = from_root(schur[:, offset_col : offset_col + PANEL], "col", owner_col)
        diagonal = from_root(panel[offset_row : offset_row + PANEL], "row", owner_row)
        lower = jnp.linalg.cholesky(diagonal)
        solved = jax.scipy.linalg.solve_triangular(lower, panel.T, lower=True).T
        row_factor = jnp.where(panel_cols > rows_global, 0.0, solved)
        source_row = col_start // row_height
        piece = lax.dynamic_slice_in_dim(row_factor, col_start % row_height, col_width, 0)
        col_factor = from_root(piece.astype(jnp.bfloat16), "row", source_row).astype(piece.dtype)
        update = lax.dot_general(
            row_factor,
            col_factor,
            over_second,
            precision=lax.Precision.HIGHEST,
            preferred_element_type=jnp.float32,
        )
        trailing = (rows_global >= stop) & (cols_global >= stop)
        schur = schur - jnp.where(trailing, update, 0.0)
        placed = jnp.pad(row_factor, ((0, 0), (offset_col, col_width - offset_col - PANEL)))
        in_panel = (cols_global >= start) & (cols_global < stop) & (rows_global >= start)
        schur = jnp.where(in_panel, placed, schur)
    return schur


def solution(mesh):
    placed = (P("row", "col"), P(None, "col"), P(None, "col"), P())
    return jax.shard_map(
        body, mesh=mesh, in_specs=placed, out_specs=P("row", "col"), check_vma=False
    )
```

profile of v0, /device:TPU:1, one launch (start us, length us, event | category | flops | bytes accessed | tf_op | source)
XLA Modules:
  0.0 1158.1 jit_solution(6297743823145924829)
XLA Ops:
  8.3 124.4 %all-reduce.22 = bf16[64,1024]{1,0:T(8,128)(2,1)} all-reduce(f32[64,1024]{1,0:T(8,128)S(1)} %fusion.29), channel_id=1, replica_groups=mesh['row'=16,'col'=32] {'col'}, use_global_device_ids=true, to_apply=%region_0.0 | all-reduce | flops 65536 | bytes 393216 | tf_op jit(solution)/shard_map/psum | solution.py:21
  134.9 62.1 %all-gather.2.cloned.1.call-done = bf16[64,16384]{1,0:T(8,128)(2,1)} async-done(((bf16[64,1024]{1,0:T(8,128)(2,1)}), bf16[64,16384]{1,0:T(8,128)(2,1)}) %all-gather.2.cloned.1.call-update) | async-done | bytes 2097168 | tf_op jit(solution)/shard_map/all_gather | solution.py:22
  197.0 4.8 copy.5
  201.8 5.6 gather_fusion
  207.4 3.8 gather_fusion.1
  213.6 156.0 %all-reduce.11.cloned.1.call-done = f32[1024,256]{0,1:T(8,128)} async-done(((f32[1024,256]{0,1:T(8,128)}), f32[1024,256]{0,1:T(8,128)}) %all-reduce.11.cloned.1.call-update) | async-done | bytes 1048592 | tf_op jit(solution)/shard_map/psum | solution.py:12
  369.6 1.7 slice_select_fusion.3
  371.9 116.8 %all-reduce.13.cloned.1.call-done = f32[256,256]{0,1:T(8,128)} async-done(((f32[256,256]{0,1:T(8,128)}), f32[256,256]{0,1:T(8,128)}) %all-reduce.13.cloned.1.call-update) | async-done | bytes 262160 | tf_op jit(solution)/shard_map/psum | solution.py:12
  491.5 11.7 %cholesky.130 = f32[128,128]{1,0:T(8,128)S(1)} custom-call(f32[128,128]{1,0:T(8,128)S(1)} %cholesky.194), custom_call_target="Cholesky" | custom-call | tf_op jit(solution)/shard_map/jit(cholesky)/cholesky | solution.py:53
  503.9 10.6 custom-call.13
  515.6 1.7 convolution_subtract_fusion.3
  517.3 12.5 %cholesky.147 = f32[128,128]{1,0:T(8,128)S(1)} custom-call(f32[128,128]{1,0:T(8,128)} %convolution_subtract_fusion.3), custom_call_target="Cholesky" | custom-call | tf_op jit(solution)/shard_map/jit(cholesky)/cholesky | solution.py:53
  533.6 5.5 while.4
  534.5 2.0 bitcast_dynamic-update-slice_fusion.4
  537.1 2.0 bitcast_dynamic-update-slice_fusion.4
  539.1 21.1 %custom-call.14 = f32[2,128,128]{1,2,0:T(8,128)} custom-call(f32[2,128,128]{2,1,0:T(8,128)} %get-tuple-element.21), custom_call_target="InvertDiagBlocksLowerTriangular" | custom-call | tf_op jit(solution)/shard_map/jit(_solve_triangular)/triangular_solve | solution.py:54
  560.2 1.5 fusion.4
  564.0 116.2 %all-reduce.15.cloned.1.call-done = bf16[512,256]{0,1:T(8,128)(2,1)} async-done(((bf16[512,256]{0,1:T(8,128)(2,1)}), bf16[512,256]{0,1:T(8,128)(2,1)}) %all-reduce.15.cloned.1.call-update) | async-done | bytes 262160 | tf_op jit(solution)/shard_map/psum | solution.py:12
  680.2 2.5 subtract_select_fusion.1
  685.2 158.4 %all-reduce.17.cloned.1.call-done = f32[1024,256]{0,1:T(8,128)} async-done(((f32[1024,256]{0,1:T(8,128)}), f32[1024,256]{0,1:T(8,128)}) %all-reduce.17.cloned.1.call-update) | async-done | bytes 1048592 | tf_op jit(solution)/shard_map/psum | solution.py:12
  843.6 1.7 slice_select_fusion.2
  845.6 117.0 %all-reduce.19.cloned.1.call-done = f32[256,256]{0,1:T(8,128)} async-done(((f32[256,256]{0,1:T(8,128)}), f32[256,256]{0,1:T(8,128)}) %all-reduce.19.cloned.1.call-update) | async-done | bytes 262160 | tf_op jit(solution)/shard_map/psum | solution.py:12
  964.7 11.7 %cholesky.164 = f32[128,128]{1,0:T(8,128)S(1)} custom-call(f32[128,128]{1,0:T(8,128)S(1)} %cholesky.197), custom_call_target="Cholesky" | custom-call | tf_op jit(solution)/shard_map/jit(cholesky)/cholesky | solution.py:53
  976.5 9.8 custom-call.15
  986.8 11.7 %cholesky.181 = f32[128,128]{1,0:T(8,128)S(1)} custom-call(f32[128,128]{1,0:T(8,128)S(1)} %convolution_subtract_fusion.2), custom_call_target="Cholesky" | custom-call | tf_op jit(solution)/shard_map/jit(cholesky)/cholesky | solution.py:53
  1001.2 4.3 while.5
  1002.1 1.3 bitcast_dynamic-update-slice_fusion.5
  1004.2 1.3 bitcast_dynamic-update-slice_fusion.5
  1005.5 19.7 %custom-call.16 = f32[2,128,128]{1,2,0:T(8,128)S(1)} custom-call(f32[2,128,128]{2,1,0:T(8,128)S(1)} %get-tuple-element.22), custom_call_target="InvertDiagBlocksLowerTriangular" | custom-call | tf_op jit(solution)/shard_map/jit(_solve_triangular)/triangular_solve | solution.py:54
  1028.0 116.3 %all-reduce.21.cloned.1.call-done = bf16[512,256]{0,1:T(8,128)(2,1)} async-done(((bf16[512,256]{0,1:T(8,128)(2,1)}), bf16[512,256]{0,1:T(8,128)(2,1)}) %all-reduce.21.cloned.1.call-update) | async-done | bytes 262160 | tf_op jit(solution)/shard_map/psum | solution.py:12
  1144.3 3.8 subtract_select_fusion
  1148.1 2.9 copy.13
  (89 shorter events, 28.3 us)
Async XLA Ops:
  6.5 0.8 copy-start
  6.5 190.5 %all-gather.2.cloned.1.call-start = ((), (), s32[]{:S(2)}) async-start(), calls=%async_computation | async-start | bytes 2228224 | tf_op jit(solution)/shard_map/all_gather | solution.py:22
  132.7 236.9 %all-reduce.11.cloned.1.call-start = ((), (), s32[]{:S(2)}) async-start(), calls=%async_computation.1 | async-start | bytes 2097152 | tf_op jit(solution)/shard_map/psum | solution.py:12
  213.6 275.2 %all-reduce.13.cloned.1.call-start = ((), (), s32[]{:S(2)}) async-start(), calls=%async_computation.2 | async-start | bytes 524288 | tf_op jit(solution)/shard_map/psum | solution.py:12
  371.3 188.9 %copy-start.3 = (f32[1024,256]{0,1:T(8,128)S(1)}, f32[1024,256]{0,1:T(8,128)}, u32[]{:S(2)}) copy-start(f32[1024,256]{0,1:T(8,128)} %all-reduce.11.cloned.1.call-done) | copy-start | bytes 3145732
  371.3 308.9 %all-reduce.15.cloned.1.call-start = ((), (), s32[]{:S(2)}) async-start(), calls=%async_computation.3 | async-start | bytes 524288 | tf_op jit(solution)/shard_map/psum | solution.py:12
  490.8 0.7 copy-start.6
  529.9 2.0 copy-start.5
  560.2 2.1 copy-start.7
  563.9 279.7 %all-reduce.17.cloned.1.call-start = ((), (), s32[]{:S(2)}) async-start(), calls=%async_computation.4 | async-start | bytes 2097152 | tf_op jit(solution)/shard_map/psum | solution.py:12
  682.7 1.3 copy-start.1
  685.1 277.5 %all-reduce.19.cloned.1.call-start = ((), (), s32[]{:S(2)}) async-start(), calls=%async_computation.5 | async-start | bytes 524288 | tf_op jit(solution)/shard_map/psum | solution.py:12
  845.3 179.9 %copy-start.4 = (f32[1024,256]{0,1:T(8,128)S(1)}, f32[1024,256]{0,1:T(8,128)}, u32[]{:S(2)}) copy-start(f32[1024,256]{0,1:T(8,128)} %all-reduce.17.cloned.1.call-done) | copy-start | bytes 3145732
  845.3 299.0 %all-reduce.21.cloned.1.call-start = ((), (), s32[]{:S(2)}) async-start(), calls=%async_computation.6 | async-start | bytes 524288 | tf_op jit(solution)/shard_map/psum | solution.py:12
  1026.4 117.9 %copy-start.2 = (f32[1024,512]{0,1:T(8,128)S(1)}, f32[1024,512]{0,1:T(8,128)}, u32[]{:S(2)}) copy-start(f32[1024,512]{0,1:T(8,128)} %copy-done.1) | copy-start | bytes 6291460
Sparse Core Ops, SparseCore 0:
  132.8 64.1 all-gather.1
  213.7 155.8 all-reduce.10
  371.9 116.7 all-reduce.12
  564.0 116.1 all-reduce.14
  685.3 158.2 all-reduce.16
  845.8 116.7 all-reduce.18
  1028.1 116.1 all-reduce.20
where the time goes:
time: 1160 us
  waiting for transfers between devices  843 us (73%)
  other arithmetic  125 us (11%)
  blocking collectives  124 us (11%)
  local copies, waits for them, and re-layouts  32.2 us (3%)
  between operations  16.7 us (1%)
  matrix products  15.9 us (1%)
    psum x6, waiting for transfers between devices, from_root(): return lax.psum(block, axis)  781 us
    psum x1, blocking collectives, body(): summed = lax.psum(partial_value, 'col')  124 us
    another operation x13, other arithmetic, body(): lower = jnp.linalg.cholesky(diagonal)  70.9 us
    all_gather x1, waiting for transfers between devices, body(): lax.all_gather(summed.astype(jnp.bfloat16), 'row', axis=1, tiled=True)  62.1 us
    another operation x5, other arithmetic, body(): solved = jax.scipy.linalg.solve_triangular(lower, panel.T, lower=True).T  41.8 us
  transfers between devices with their start and end apart: 7, of which 7 were waited for; matrix products, arithmetic and copies ran while one was open for 0% of the time, Pallas kernels for 0%

commit v1 on v0

v1 whole, which is shorter than its diff:
```python
import functools

import jax
import jax.numpy as jnp
from jax import lax
from jax.experimental import pallas as pl
from jax.experimental.pallas import tpu as pltpu
from jax.sharding import PartitionSpec as P

F32 = jnp.float32
HI = lax.Precision.HIGHEST
NT = (((1,), (1,)), ((), ()))


def factor_block(load, store, lanes, subs):
    A = [load(t) for t in range(16)]
    for t in range(16):
        j0 = 8 * t
        C = {}
        for s in range(t, 16):
            for i in range(8):
                C[s, i] = jnp.broadcast_to(A[s][:, j0 + i : j0 + i + 1], (8, 128))
        for s in range(t + 1, 16):
            A[s] = jnp.where((lanes >= j0) & (lanes < j0 + 8), 0.0, A[s])
        R = A[t]
        piv = jnp.zeros((8, 128), F32)
        for i in range(8):
            p = jnp.broadcast_to(C[t, i][i : i + 1, :], (8, 128))
            ip = 1.0 / p
            piv = jnp.where(subs == i, p, piv)
            Ri = jnp.broadcast_to(R[i : i + 1, :], (8, 128))
            Ri = jnp.where(lanes == j0 + i, 1.0, Ri)
            rows = {l: jnp.broadcast_to(C[t, l][i : i + 1, :], (8, 128)) for l in range(i + 1, 8)}
            Rs = jnp.where((lanes > j0 + i) & (lanes < j0 + 8), 0.0, Ri)
            m = jnp.where(subs > i, C[t, i] * ip, 0.0)
            R = jnp.where((subs > i) & (lanes == j0 + i), 0.0, R) - m * Ri
            for l in range(i + 1, 8):
                C[t, l] = C[t, l] - m * rows[l]
            for s in range(t + 1, 16):
                m = C[s, i] * ip
                A[s] = A[s] - m * Rs
                for l in range(i + 1, 8):
                    C[s, l] = C[s, l] - m * rows[l]
        rs = lax.rsqrt(piv)
        inv = jnp.where(lanes < j0 + subs, R * rs, jnp.where(lanes == j0 + subs, rs, 0.0))
        store(t, inv)


def kernel(rc, idx_ref, tab_ref, out_ref, t2, g32, gu, gv, sx, inv_ref):
    r, c = rc() if callable(rc) else rc
    lanes = lax.broadcasted_iota(jnp.int32, (8, 128), 1)
    subs = lax.broadcasted_iota(jnp.int32, (8, 128), 0)

    def unpack(b, _):
        src = pl.multiple_of(b * 512, 512)
        for q in range(16):
            v = tab_ref[pl.ds(src + q * 32, 32), :].astype(F32)
            dst = pl.multiple_of(b * 1024, 1024)
            t2[pl.ds(dst + q * 32, 32), :] = v
            t2[pl.ds(dst + 512 + q * 32, 32), :] = pltpu.roll(v, 64, 1)
        return 0

    lax.fori_loop(0, 16, unpack, 0)

    def pick(n, base, dst):
        def body(i, _):
            for q in range(16):
                j = i * 16 + q
                g32[pl.ds(dst + j, 1), :] = t2[pl.ds(idx_ref[base + j], 1), :]
            return 0
        lax.fori_loop(0, n // 16, body, 0)

    pick(512, 0, 0)
    pick(512, c * 512, 512)
    pick(1024, r * 1024, 1024)
    wide = lax.broadcasted_iota(jnp.int32, (256, 128), 1)

    def masks(i, _):
        rows = pl.ds(pl.multiple_of(i * 256, 256), 256)
        g = g32[rows, :]
        gu[rows, :] = jnp.where(wide < 32, g, 0.0).astype(jnp.bfloat16)
        gv[rows, :] = jnp.where((wide >= 32) & (wide < 64), g, 0.0).astype(jnp.bfloat16)
        return 0

    lax.fori_loop(0, 8, masks, 0)

    def gram(rows, cols):
        a = lax.dot_general(gu[rows, :], gu[cols, :], NT, preferred_element_type=F32)
        b = lax.dot_general(gv[rows, :], gv[cols, :], NT, preferred_element_type=F32)
        return a * b

    il = lax.broadcasted_iota(jnp.int32, (256, 512), 0)
    ic = lax.broadcasted_iota(jnp.int32, (256, 512), 1)
    for i in range(8):
        rows = pl.ds(i * 256, 256)
        first = i * 256 if i < 2 else (c * 512 + (i - 2) * 256 if i < 4 else r * 1024 + (i - 4) * 256)
        sx[rows, :] = gram(rows, pl.ds(0, 512)) + jnp.where(il + first == ic, 1.0, 0.0)

    for k in range(4):
        cols = pl.ds(k * 128, 128)
        factor_block(
            lambda t: sx[pl.ds(k * 128 + 8 * t, 8), cols],
            lambda t, v: inv_ref.__setitem__((pl.ds(8 * t, 8), slice(None)), v),
            lanes, subs,
        )
        for i in range(8):
            rows = pl.ds(i * 256, 256)
            if i * 256 + 256 <= k * 128:
                continue
            sx[rows, cols] = lax.dot_general(sx[rows, cols], inv_ref[...], NT, precision=HI, preferred_element_type=F32)
        if k < 3:
            rest = pl.ds(k * 128 + 128, 384 - k * 128)
            for i in range(8):
                if i * 256 + 256 <= k * 128 + 128:
                    continue
                rows = pl.ds(i * 256, 256)
                sx[rows, rest] = sx[rows, rest] - lax.dot_general(
                    sx[rows, cols], sx[rest, cols], NT, precision=HI, preferred_element_type=F32)

    for i in range(4):
        rows = pl.ds(1024 + i * 256, 256)
        dst = pl.ds(i * 256, 256)
        grow = il + (r * 1024 + i * 256)
        s = gram(rows, pl.ds(512, 512)) + jnp.where(grow == ic + c * 512, 1.0, 0.0)
        b = sx[rows, :]

        @pl.when(c == 0)
        def _():
            lead = jnp.where(ic <= grow, b, jnp.where((grow < 256) & (ic >= 256), s, 0.0))
            out_ref[dst, :] = jnp.where(grow < 512, lead, b)

        @pl.when(c != 0)
        def _():
            keep = (grow >= 512) | ((grow >= 256) & (ic < 256))
            bm = jnp.where(keep, b, 0.0)
            out_ref[dst, :] = s - lax.dot_general(bm, sx[pl.ds(512, 512), :], NT, precision=HI, preferred_element_type=F32)


def local_part(rc):
    def f(idx, tab):
        return pl.pallas_call(
            functools.partial(kernel, rc),
            out_shape=jax.ShapeDtypeStruct((1024, 512), F32),
            in_specs=[pl.BlockSpec(memory_space=pltpu.SMEM), pl.BlockSpec(memory_space=pltpu.VMEM)],
            out_specs=pl.BlockSpec(memory_space=pltpu.VMEM),
            scratch_shapes=[
                pltpu.VMEM((16384, 128), F32),
                pltpu.VMEM((2048, 128), F32),
                pltpu.VMEM((2048, 128), jnp.bfloat16),
                pltpu.VMEM((2048, 128), jnp.bfloat16),
                pltpu.VMEM((2048, 512), F32),
                pltpu.VMEM((128, 128), F32),
            ],
            compiler_params=pltpu.CompilerParams(vmem_limit_bytes=60 << 20),
        )(idx, tab)
    return f


MESH = pl.DeviceIdType.MESH
BF16 = jnp.bfloat16


def share_kernel(nx, nz, ny, x_ref, u_ref, v_ref, out_ref, part, rx, sumx, rz, tab,
                 rx_s, rx_r, rz_s, rz_r, az_s, az_r, ax_s, ax_r, yp_s, yp_r, ym_s, ym_r, pc_s, pc_r, out_sem):
    row, col = lax.axis_index("row"), lax.axis_index("col")
    y, core = row // 2, row % 2
    x, z = col // nz, col % nz
    twin = row + 1 - 2 * core

    def at_x(d):
        return (row, (x + d) % nx * nz + z)

    def at_z(d):
        return (row, x * nz + (z + d) % nz)

    def at_y(d):
        return ((y + d) % ny * 2 + core, col)

    barrier = pltpu.get_barrier_semaphore()
    peers = [at_x(d) for d in range(1, nx)] + [at_z(d) for d in range(1, nz)] + [at_y(1), at_y(ny - 1), (twin, col)]
    for peer in peers:
        pl.semaphore_signal(barrier, inc=1, device_id=peer, device_id_type=MESH)

    def copy(src, dst, send, recv, peer):
        return pltpu.make_async_remote_copy(
            src_ref=src, dst_ref=dst, send_sem=send, recv_sem=recv, device_id=peer, device_id_type=MESH)

    u, v = u_ref[...], v_ref[...]
    zero = jnp.zeros_like(u)
    half = x_ref.shape[0] // 2
    low = jnp.concatenate([u, v, zero, zero], axis=0)
    high = jnp.concatenate([zero, zero, u, v], axis=0)
    both = lax.dot_general(x_ref[:half, :], low, NT, preferred_element_type=F32)
    both = both + lax.dot_general(x_ref[half:, :], high, NT, preferred_element_type=F32)
    part[...] = both.reshape(part.shape)
    pl.semaphore_wait(barrier, len(peers))

    sent = []

    def go(c):
        c.start()
        sent.append(c)

    for d in range(1, nx):
        go(copy(part.at[(x + d) % nx], rx.at[d - 1], rx_s.at[d - 1], rx_r.at[d - 1], at_x(d)))
    total = part[x]
    for d in range(1, nx):
        copy(part.at[x], rx.at[d - 1], rx_s.at[d - 1], rx_r.at[d - 1], at_x(d)).wait_recv()
        total = total + rx[d - 1]
    sumx[...] = total
    for d in range(1, nz):
        go(copy(sumx.at[(z + d) % nz], rz.at[d - 1], rz_s.at[d - 1], rz_r.at[d - 1], at_z(d)))
    tile = sumx[z]
    for d in range(1, nz):
        copy(sumx.at[z], rz.at[d - 1], rz_s.at[d - 1], rz_r.at[d - 1], at_z(d)).wait_recv()
        tile = tile + rz[d - 1]
    tab[row, x, z] = tile.astype(BF16)

    for d in range(1, nz):
        mine = tab.at[row, x, z]
        go(copy(mine, mine, az_s.at[d - 1], az_r.at[d - 1], at_z(d)))
    for d in range(1, nz):
        theirs = tab.at[row, x, (z + nz - d) % nz]
        copy(theirs, theirs, az_s.at[d - 1], az_r.at[d - 1], at_z(d)).wait_recv()
    for d in range(1, nx):
        mine = tab.at[row, x]
        go(copy(mine, mine, ax_s.at[d - 1], ax_r.at[d - 1], at_x(d)))

    def piece(away, e):
        return tab.at[(y + ny - away) % ny * 2 + core, (x + nx - e) % nx]

    def arrived(k, e, away):
        ref = piece(away, e)
        go(copy(ref, ref, pc_s.at[k, e], pc_r.at[k, e], (twin, col)))

    up, down = ny // 2, ny - 1 - ny // 2

    def reach(e):
        return (up, down) if e % 2 == 0 else (down, up)

    for e in range(nx):
        if e:
            theirs = piece(0, e)
            copy(theirs, theirs, ax_s.at[e - 1], ax_r.at[e - 1], at_x(e)).wait_recv()
        ref = piece(0, e)
        go(copy(ref, ref, yp_s.at[0, e], yp_r.at[0, e], at_y(1)))
        go(copy(ref, ref, ym_s.at[0, e], ym_r.at[0, e], at_y(ny - 1)))
        arrived(0, e, 0)
    for s in range(1, up + 1):
        for e in range(nx):
            plus, minus = reach(e)
            if s <= plus:
                ref = piece(s, e)
                copy(ref, ref, yp_s.at[s - 1, e], yp_r.at[s - 1, e], at_y(1)).wait_recv()
                if s < plus:
                    go(copy(ref, ref, yp_s.at[s, e], yp_r.at[s, e], at_y(1)))
                arrived(s, e, s)
            if s <= minus:
                ref = piece(ny - s, e)
                copy(ref, ref, ym_s.at[s - 1, e], ym_r.at[s - 1, e], at_y(ny - 1)).wait_recv()
                if s < minus:
                    go(copy(ref, ref, ym_s.at[s, e], ym_r.at[s, e], at_y(ny - 1)))
                arrived(ny - s, e, ny - s)
    for k in range(ny):
        for e in range(nx):
            ref = tab.at[(y + ny - k) % ny * 2 + 1 - core, (x + nx - e) % nx]
            copy(ref, ref, pc_s.at[k, e], pc_r.at[k, e], (twin, col)).wait_recv()
    done = pltpu.make_async_copy(tab, out_ref, out_sem)
    done.start()
    for c in sent:
        c.wait_send()
    done.wait()


def share(nx, nz, ny, vectors, u, v):
    rows = vectors.shape[0] // 2
    block = rows // (nx * nz)
    dma = pltpu.SemaphoreType.DMA
    tab = (2 * ny, nx, nz, block, 128)
    vm = pl.BlockSpec(memory_space=pltpu.VMEM)
    pairs = []
    for shape in ((nx - 1,), (nz - 1,), (nz - 1,), (nx - 1,), (ny // 2, nx), (ny // 2, nx), (ny, nx)):
        pairs += [dma(shape), dma(shape)]
    return pl.pallas_call(
        functools.partial(share_kernel, nx, nz, ny),
        out_shape=jax.ShapeDtypeStruct(tab, BF16),
        in_specs=[vm] * 3,
        out_specs=pl.BlockSpec(memory_space=pl.ANY),
        scratch_shapes=[
            pltpu.VMEM((nx, nz, block, 128), F32),
            pltpu.VMEM((nx - 1, nz, block, 128), F32),
            pltpu.VMEM((nz, block, 128), F32),
            pltpu.VMEM((nz - 1, block, 128), F32),
            pltpu.VMEM(tab, BF16),
        ] + pairs + [dma],
        compiler_params=pltpu.CompilerParams(collective_id=0, has_side_effects=True, vmem_limit_bytes=32 << 20),
    )(vectors, u, v)


def body(outcome_vectors, u_factor, v_factor, outcome_index):
    table = share(4, 8, 8, outcome_vectors, u_factor, v_factor)
    return local_part(lambda: (lax.axis_index("row"), lax.axis_index("col")))(outcome_index, table.reshape(-1, 128))


def solution(mesh):
    placed = (P("row", "col"), P(None, "col"), P(None, "col"), P())
    return jax.shard_map(
        body, mesh=mesh, in_specs=placed, out_specs=P("row", "col"), check_vma=False
    )
```

time: 1160 us -> 87.3 us (0.08)
  the two profiles are of different devices: /device:TPU:1 before, /device:TPU:3 now
where the time goes in v1:
time: 87.3 us; the launch traced here: 87.1 us
  Pallas kernels  83.3 us (95%)
  local copies, waits for them, and re-layouts  3.73 us (4%)
    pallas_call x1, Pallas kernels, share(): pl.pallas_call(functools.partial(share_kernel, nx, nz, ny), out_shape=jax...  48.2 us
    pallas_call x1, Pallas kernels, f(): pl.pallas_call(functools.partial(kernel, rc), out_shape=jax.ShapeDtypeStr...  35.1 us
    unnamed x7, local copies, waits for them, and re-layouts  3.73 us

profile of v1, /device:TPU:3, one launch (start us, length us, event | category | flops | bytes accessed | tf_op | source)
XLA Modules:
  0.0 87.1 jit_solution(12740190219132564286)
XLA Ops:
  0.0 1.0 %copy.5.x_ref = bf16[1024,32]{1,0:T(8,128)(2,1)S(1)} copy(bf16[1024,32]{0,1:T(8,128)(2,1)} %param.4) | data formatting | bytes 131072 | tf_op args[0]
  1.0 0.0 copy-start.1
  1.0 0.7 copy-done.1
  1.7 0.0 copy-start.2
  1.7 0.7 copy-done.2
  2.4 48.2 %shard_map.46 = bf16[16,4,8,16,128]{4,3,2,1,0:T(8,128)(2,1)S(1)} custom-call(bf16[1024,32]{1,0:T(8,128)(2,1)S(1)} %copy.5.x_ref, bf16[32,32]{1,0:T(8,128)(2,1)S(1)} %copy-done.1, bf16[32,32]{1,0:T(8,128)(2,1)S(1)} %copy-done.2), custom_call_target="tpu_custom_call" | custom-call | tf_op jit(solution)/shard_map/pallas_call | solution.py:284
  50.6 0.0 copy-start
  50.6 1.3 %copy-done = bf16[16,4,8,16,128]{4,3,2,1,0:T(8,128)(2,1)} copy-done((bf16[16,4,8,16,128]{4,3,2,1,0:T(8,128)(2,1)}, bf16[16,4,8,16,128]{4,3,2,1,0:T(8,128)(2,1)S(1)}, u32[]{:S(2)}) %copy-start) | copy-done | bytes 2097176
  52.0 35.1 %shard_map.47 = f32[1024,512]{1,0:T(8,128)} custom-call(s32[16384]{0:T(1024)} %idx_ref.1, bf16[8192,128]{1,0:T(8,128)(2,1)} %bitcast.1), custom_call_target="tpu_custom_call" | custom-call | tf_op jit(solution)/shard_map/pallas_call | solution.py:141
Async XLA Ops:
  1.0 0.7 copy-start.1
  1.7 0.7 copy-start.2
  50.6 1.3 %copy-start = (bf16[16,4,8,16,128]{4,3,2,1,0:T(8,128)(2,1)}, bf16[16,4,8,16,128]{4,3,2,1,0:T(8,128)(2,1)S(1)}, u32[]{:S(2)}) copy-start(bf16[16,4,8,16,128]{4,3,2,1,0:T(8,128)(2,1)S(1)} %shard_map.46) | copy-start | bytes 6291460

commit v2 on v1

v2 whole, which is shorter than its diff:
```python
import functools

import jax
import jax.numpy as jnp
from jax import lax
from jax.experimental import pallas as pl
from jax.experimental.pallas import tpu as pltpu
from jax.sharding import PartitionSpec as P

F32 = jnp.float32
HI = lax.Precision.HIGHEST
NT = (((1,), (1,)), ((), ()))


def factor_block(load, store, lanes, subs):
    A = [load(t) for t in range(16)]
    for t in range(16):
        j0 = 8 * t
        C = {}
        for s in range(t, 16):
            for i in range(8):
                C[s, i] = jnp.broadcast_to(A[s][:, j0 + i : j0 + i + 1], (8, 128))
        for s in range(t + 1, 16):
            A[s] = jnp.where((lanes >= j0) & (lanes < j0 + 8), 0.0, A[s])
        R = A[t]
        piv = jnp.zeros((8, 128), F32)
        for i in range(8):
            p = jnp.broadcast_to(C[t, i][i : i + 1, :], (8, 128))
            ip = 1.0 / p
            piv = jnp.where(subs == i, p, piv)
            Ri = jnp.broadcast_to(R[i : i + 1, :], (8, 128))
            Ri = jnp.where(lanes == j0 + i, 1.0, Ri)
            rows = {l: jnp.broadcast_to(C[t, l][i : i + 1, :], (8, 128)) for l in range(i + 1, 8)}
            Rs = jnp.where((lanes > j0 + i) & (lanes < j0 + 8), 0.0, Ri)
            m = jnp.where(subs > i, C[t, i] * ip, 0.0)
            R = jnp.where((subs > i) & (lanes == j0 + i), 0.0, R) - m * Ri
            for l in range(i + 1, 8):
                C[t, l] = C[t, l] - m * rows[l]
            for s in range(t + 1, 16):
                m = C[s, i] * ip
                A[s] = A[s] - m * Rs
                for l in range(i + 1, 8):
                    C[s, l] = C[s, l] - m * rows[l]
        rs = lax.rsqrt(piv)
        inv = jnp.where(lanes < j0 + subs, R * rs, jnp.where(lanes == j0 + subs, rs, 0.0))
        store(t, inv)


def split(x):
    high = x.astype(jnp.bfloat16)
    return high, (x - high.astype(F32)).astype(jnp.bfloat16)


def dot(a, b):
    return lax.dot_general(a, b, NT, preferred_element_type=F32)


def kernel(rc, idx_ref, tab_ref, out_ref, t2, g32, gu, gv, sx, inv_ref, ch, cl):
    r, c = rc() if callable(rc) else rc
    lanes = lax.broadcasted_iota(jnp.int32, (8, 128), 1)
    subs = lax.broadcasted_iota(jnp.int32, (8, 128), 0)

    def unpack(b, _):
        for core in range(2):
            for x in range(4):
                for a in range(8):
                    y, z = (a, b) if core == 0 else (b, a)
                    tile = tab_ref[core, b, x, a].astype(F32)
                    dst = pl.multiple_of((y * 2 + core) * 1024 + (x * 8 + z) * 16, 16)
                    t2[pl.ds(dst, 16), :] = tile
                    t2[pl.ds(dst + 512, 16), :] = pltpu.roll(tile, 64, 1)
        return 0

    lax.fori_loop(0, 8, unpack, 0)

    def pick(n, base, dst):
        def body(i, _):
            for q in range(16):
                j = i * 16 + q
                g32[pl.ds(dst + j, 1), :] = t2[pl.ds(idx_ref[base + j], 1), :]
            return 0
        lax.fori_loop(0, n // 16, body, 0)

    pick(512, 0, 0)
    pick(512, c * 512, 512)
    pick(1024, r * 1024, 1024)
    wide = lax.broadcasted_iota(jnp.int32, (256, 128), 1)

    def masks(i, _):
        rows = pl.ds(pl.multiple_of(i * 256, 256), 256)
        g = g32[rows, :]
        gu[rows, :] = jnp.where(wide < 32, g, 0.0).astype(jnp.bfloat16)
        gv[rows, :] = jnp.where((wide >= 32) & (wide < 64), g, 0.0).astype(jnp.bfloat16)
        return 0

    lax.fori_loop(0, 8, masks, 0)

    def gram(rows, cols):
        a = lax.dot_general(gu[rows, :], gu[cols, :], NT, preferred_element_type=F32)
        b = lax.dot_general(gv[rows, :], gv[cols, :], NT, preferred_element_type=F32)
        return a * b

    il = lax.broadcasted_iota(jnp.int32, (256, 512), 0)
    ic = lax.broadcasted_iota(jnp.int32, (256, 512), 1)
    for i in range(8):
        rows = pl.ds(i * 256, 256)
        first = i * 256 if i < 2 else (c * 512 + (i - 2) * 256 if i < 4 else r * 1024 + (i - 4) * 256)
        sx[rows, :] = gram(rows, pl.ds(0, 512)) + jnp.where(il + first == ic, 1.0, 0.0)

    for k in range(4):
        cols = pl.ds(k * 128, 128)
        factor_block(
            lambda t: sx[pl.ds(k * 128 + 8 * t, 8), cols],
            lambda t, v: inv_ref.__setitem__((pl.ds(8 * t, 8), slice(None)), v),
            lanes, subs,
        )
        for i in range(8):
            rows = pl.ds(i * 256, 256)
            if i * 256 + 256 <= k * 128:
                continue
            sx[rows, cols] = lax.dot_general(sx[rows, cols], inv_ref[...], NT, precision=HI, preferred_element_type=F32)
        if k < 3:
            rest = pl.ds(k * 128 + 128, 384 - k * 128)
            for i in range(8):
                if i * 256 + 256 <= k * 128 + 128:
                    continue
                rows = pl.ds(i * 256, 256)
                sx[rows, rest] = sx[rows, rest] - lax.dot_general(
                    sx[rows, cols], sx[rest, cols], NT, precision=HI, preferred_element_type=F32)

    ch[...], cl[...] = split(sx[pl.ds(512, 512), :])
    for i in range(4):
        rows = pl.ds(1024 + i * 256, 256)
        dst = pl.ds(i * 256, 256)
        grow = il + (r * 1024 + i * 256)
        s = gram(rows, pl.ds(512, 512)) + jnp.where(grow == ic + c * 512, 1.0, 0.0)
        b = sx[rows, :]

        @pl.when(c == 0)
        def _():
            lead = jnp.where(ic <= grow, b, jnp.where((grow < 256) & (ic >= 256), s, 0.0))
            out_ref[dst, :] = jnp.where(grow < 512, lead, b)

        @pl.when(c != 0)
        def _():
            keep = (grow >= 512) | ((grow >= 256) & (ic < 256))
            bm = jnp.where(keep, b, 0.0)
            bh, bl = split(bm)
            out_ref[dst, :] = s - (dot(bh, ch[...]) + (dot(bh, cl[...]) + dot(bl, ch[...])))


def local_part(rc):
    def f(idx, tab):
        return pl.pallas_call(
            functools.partial(kernel, rc),
            out_shape=jax.ShapeDtypeStruct((1024, 512), F32),
            in_specs=[pl.BlockSpec(memory_space=pltpu.SMEM), pl.BlockSpec(memory_space=pltpu.VMEM)],
            out_specs=pl.BlockSpec(memory_space=pltpu.VMEM),
            scratch_shapes=[
                pltpu.VMEM((16384, 128), F32),
                pltpu.VMEM((2048, 128), F32),
                pltpu.VMEM((2048, 128), jnp.bfloat16),
                pltpu.VMEM((2048, 128), jnp.bfloat16),
                pltpu.VMEM((2048, 512), F32),
                pltpu.VMEM((128, 128), F32),
                pltpu.VMEM((512, 512), jnp.bfloat16),
                pltpu.VMEM((512, 512), jnp.bfloat16),
            ],
            compiler_params=pltpu.CompilerParams(vmem_limit_bytes=24 << 20),
        )(idx, tab)
    return f


MESH = pl.DeviceIdType.MESH
BF16 = jnp.bfloat16

def share_kernel(nx, n, x_ref, u_ref, v_ref, tab, xs, fs, sumx, rz, mine,
                 own_s, xs_s, xs_r, rz_s, rz_r, aa_s, aa_r, ax_s, ax_r, bp_s, bp_r, bm_s, bm_r, tw_s, tw_r):
    row, col = lax.axis_index("row"), lax.axis_index("col")
    y, core = row // 2, row % 2
    x, z = col // n, col % n
    other = 1 - core
    a, b = y * other + z * core, z * other + y * core
    twin = (row + 1 - 2 * core, col)

    def at_x(d):
        return (row, (x + d) % nx * n + z)

    def at_z(d):
        return (row, x * n + (z + d) % n)

    def at_y(d):
        return ((y + d) % n * 2 + core, col)

    def at_a(d):
        return (((y + d * other) % n) * 2 + core, x * n + (z + d * core) % n)

    def at_b(d):
        return (((y + d * core) % n) * 2 + core, x * n + (z + d * other) % n)

    barrier = pltpu.get_barrier_semaphore()
    peers = [at_x(d) for d in range(1, nx)] + [f(d) for f in (at_z, at_y) for d in range(1, n)] + [twin]
    for peer in peers:
        pl.semaphore_signal(barrier, inc=1, device_id=peer, device_id_type=MESH)

    def copy(src, dst, send, recv, peer):
        return pltpu.make_async_remote_copy(
            src_ref=src, dst_ref=dst, send_sem=send, recv_sem=recv, device_id=peer, device_id_type=MESH)

    half = x_ref.shape[1] // 2
    wide = half // nx

    def slices(to):
        lanes = pl.multiple_of(to * wide, wide)
        return [x_ref.at[:, pl.ds(lanes, wide)], x_ref.at[:, pl.ds(half + lanes, wide)], u_ref, v_ref]

    def slots(d):
        return [xs.at[d, 0], xs.at[d, 1], fs.at[d, 0], fs.at[d, 1]]

    own = [pltpu.make_async_copy(s, t, own_s.at[i]) for i, (s, t) in enumerate(zip(slices(x), slots(0)))]
    for c in own:
        c.start()
    pl.semaphore_wait(barrier, len(peers))

    sent = []

    def go(c):
        c.start()
        sent.append(c)

    def finish():
        for c in sent:
            c.wait_send()

    for d in range(1, nx):
        for i, (s, t) in enumerate(zip(slices((x + d) % nx), slots(d))):
            go(copy(s, t, xs_s.at[d - 1, i], xs_r.at[d - 1, i], at_x(d)))
    for c in own:
        c.wait()

    def product(d):
        f = fs[d].reshape(-1, fs.shape[-1])
        zero = jnp.zeros_like(f)
        over = (((0,), (1,)), ((), ()))
        return lax.dot_general(xs[d, 0], jnp.concatenate([f, zero], axis=0), over, preferred_element_type=F32) + \
            lax.dot_general(xs[d, 1], jnp.concatenate([zero, f], axis=0), over, preferred_element_type=F32)

    total = product(0)
    for d in range(1, nx):
        for i, (s, t) in enumerate(zip(slices(x), slots(d))):
            copy(s, t, xs_s.at[d - 1, i], xs_r.at[d - 1, i], at_x(d)).wait_recv()
        total = total + product(d)
    sumx[...] = total.reshape(sumx.shape)

    for d in range(1, n):
        go(copy(sumx.at[(z + d) % n], rz.at[d - 1], rz_s.at[d - 1], rz_r.at[d - 1], at_z(d)))
    tile = sumx[z]
    for d in range(1, n):
        copy(sumx.at[z], rz.at[d - 1], rz_s.at[d - 1], rz_r.at[d - 1], at_z(d)).wait_recv()
        tile = tile + rz[d - 1]
    mine[...] = tile.astype(BF16)

    keep = pltpu.make_async_copy(mine, tab.at[core, b, x, a], own_s.at[4])
    keep.start()
    for d in range(1, n):
        go(copy(mine, tab.at[core, b, x, a], aa_s.at[d - 1], aa_r.at[d - 1], at_a(d)))
    keep.wait()
    for d in range(1, n):
        copy(mine, tab.at[core, b, x, (a + n - d) % n], aa_s.at[d - 1], aa_r.at[d - 1], at_a(d)).wait_recv()

    def piece(away, e):
        return tab.at[core, (b + n - away) % n, (x + nx - e) % nx]

    for d in range(1, nx):
        go(copy(piece(0, 0), piece(0, 0), ax_s.at[d - 1], ax_r.at[d - 1], at_x(d)))

    def pass_on(k, e):
        go(copy(piece(k, e), piece(k, e), tw_s.at[k, e], tw_r.at[k, e], twin))

    def reach(e):
        return (n // 2, n - 1 - n // 2) if e % 2 == 0 else (n - 1 - n // 2, n // 2)

    for e in range(nx):
        if e:
            copy(piece(0, e), piece(0, e), ax_s.at[e - 1], ax_r.at[e - 1], at_x(e)).wait_recv()
        go(copy(piece(0, e), piece(0, e), bp_s.at[0, e], bp_r.at[0, e], at_b(1)))
        go(copy(piece(0, e), piece(0, e), bm_s.at[0, e], bm_r.at[0, e], at_b(n - 1)))
        pass_on(0, e)
    for s in range(1, n // 2 + 1):
        for e in range(nx):
            plus, minus = reach(e)
            for far, k, ss, rr, to in ((plus, s, bp_s, bp_r, 1), (minus, n - s, bm_s, bm_r, n - 1)):
                if s > far:
                    continue
                ref = piece(k, e)
                copy(ref, ref, ss.at[s - 1, e], rr.at[s - 1, e], at_b(to)).wait_recv()
                if s < far:
                    go(copy(ref, ref, ss.at[s, e], rr.at[s, e], at_b(to)))
                pass_on(k, e)
    theirs = z * core + y * other
    for k in range(n):
        for e in range(nx):
            ref = tab.at[other, (theirs + n - k) % n, (x + nx - e) % nx]
            copy(ref, ref, tw_s.at[k, e], tw_r.at[k, e], twin).wait_recv()
    finish()


def share(nx, n, vectors, u, v):
    depth, rows = vectors.shape
    block = rows // 2 // (nx * n)
    dma = pltpu.SemaphoreType.DMA
    tab = (2, n, nx, n, block, 128)
    hbm = pl.BlockSpec(memory_space=pltpu.MemorySpace.HBM)
    pairs = []
    for shape in ((nx - 1, 4), (n - 1,), (n - 1,), (nx - 1,), (n // 2, nx), (n // 2, nx), (n, nx)):
        pairs += [dma(shape), dma(shape)]
    return pl.pallas_call(
        functools.partial(share_kernel, nx, n),
        out_shape=jax.ShapeDtypeStruct(tab, BF16),
        in_specs=[hbm] * 3,
        out_specs=pl.BlockSpec(memory_space=pl.ANY),
        scratch_shapes=[
            pltpu.VMEM((nx, 2, depth, rows // 2 // nx), BF16),
            pltpu.VMEM((nx, 2) + u.shape, BF16),
            pltpu.VMEM((n, block, 128), F32),
            pltpu.VMEM((n - 1, block, 128), F32),
            pltpu.VMEM((block, 128), BF16),
            dma((5,)),
        ] + pairs,
        compiler_params=pltpu.CompilerParams(collective_id=0, has_side_effects=True, vmem_limit_bytes=8 << 20),
    )(vectors, u, v)


def in_hbm(t):
    return pltpu.with_memory_space_constraint(t, pltpu.MemorySpace.HBM)


def body(outcome_vectors, u_factor, v_factor, outcome_index):
    table = share(4, 8, in_hbm(outcome_vectors.T), in_hbm(u_factor), in_hbm(v_factor))
    return local_part(lambda: (lax.axis_index("row"), lax.axis_index("col")))(outcome_index, table)


def solution(mesh):
    placed = (P("row", "col"), P(None, "col"), P(None, "col"), P())
    return jax.shard_map(
        body, mesh=mesh, in_specs=placed, out_specs=P("row", "col"), check_vma=False
    )
```

time: 87.3 us -> 81.7 us (0.936)
  the two profiles are of different devices: /device:TPU:3 before, /device:TPU:1 now
where the time goes in v2:
time: 81.7 us; the launch traced here: 80.6 us
  Pallas kernels  80.5 us (99%)
    pallas_call x1, Pallas kernels, share(): pl.pallas_call(functools.partial(share_kernel, nx, n), out_shape=jax.Shap...  50 us
    pallas_call x1, Pallas kernels, f(): pl.pallas_call(functools.partial(kernel, rc), out_shape=jax.ShapeDtypeStr...  30.6 us

profile of v2, /device:TPU:1, one launch (start us, length us, event | category | flops | bytes accessed | tf_op | source)
XLA Modules:
  0.0 80.6 jit_solution(12023663109125835718)
XLA Ops:
  0.0 0.0 copy-start
  0.0 50.0 %shard_map.46.tab_ref = bf16[2,8,4,8,16,128]{5,4,3,2,1,0:T(8,128)(2,1)S(1)} custom-call(bf16[32,1024]{1,0:T(8,128)(2,1)} %bitcast.1, bf16[32,32]{1,0:T(8,128)(2,1)} %u_ref.1, bf16[32,32]{1,0:T(8,128)(2,1)} %v_ref.1), custom_call_target="tpu_custom_call" | custom-call | tf_op jit(solution)/shard_map/pallas_call | solution.py:317
  50.0 0.0 copy-done
  50.0 30.6 %shard_map.47 = f32[1024,512]{1,0:T(8,128)} custom-call(s32[16384]{0:T(1024)S(1)} %copy-done, bf16[2,8,4,8,16,128]{5,4,3,2,1,0:T(8,128)(2,1)S(1)} %shard_map.46.tab_ref), custom_call_target="tpu_custom_call" | custom-call | tf_op jit(solution)/shard_map/pallas_call | solution.py:154
Async XLA Ops:
  0.0 50.0 %copy-start = (s32[16384]{0:T(1024)S(1)}, s32[16384]{0:T(1024)}, u32[]{:S(2)}) copy-start(s32[16384]{0:T(1024)} %idx_ref.1) | copy-start | bytes 196612

commit v3 on v2

--- a/solution.py
+++ b/solution.py
@@ -12,38 +12,45 @@
 NT = (((1,), (1,)), ((), ()))
 
 
+def spread(x, j):
+    return jnp.take_along_axis(x, jnp.full((8, 128), j, jnp.int32), axis=1)
+
+
+def row_of(x, i):
+    return jnp.broadcast_to(x[i : i + 1, :], (8, 128))
+
+
 def factor_block(load, store, lanes, subs):
     A = [load(t) for t in range(16)]
     for t in range(16):
         j0 = 8 * t
-        C = {}
-        for s in range(t, 16):
-            for i in range(8):
-                C[s, i] = jnp.broadcast_to(A[s][:, j0 + i : j0 + i + 1], (8, 128))
-        for s in range(t + 1, 16):
-            A[s] = jnp.where((lanes >= j0) & (lanes < j0 + 8), 0.0, A[s])
+        inside = (lanes >= j0) & (lanes < j0 + 8)
+        C = [spread(A[t], j0 + i) for i in range(8)]
         R = A[t]
         piv = jnp.zeros((8, 128), F32)
+        rows, outer = {}, []
         for i in range(8):
-            p = jnp.broadcast_to(C[t, i][i : i + 1, :], (8, 128))
+            p = row_of(C[i], i)
             ip = 1.0 / p
             piv = jnp.where(subs == i, p, piv)
-            Ri = jnp.broadcast_to(R[i : i + 1, :], (8, 128))
-            Ri = jnp.where(lanes == j0 + i, 1.0, Ri)
-            rows = {l: jnp.broadcast_to(C[t, l][i : i + 1, :], (8, 128)) for l in range(i + 1, 8)}
-            Rs = jnp.where((lanes > j0 + i) & (lanes < j0 + 8), 0.0, Ri)
-            m = jnp.where(subs > i, C[t, i] * ip, 0.0)
+            Ri = jnp.where(lanes == j0 + i, 1.0, row_of(R, i)) * ip
+            for l in range(i + 1, 8):
+                rows[i, l] = row_of(C[l], i) * ip
+            m = jnp.where(subs > i, C[i], 0.0)
             R = jnp.where((subs > i) & (lanes == j0 + i), 0.0, R) - m * Ri
             for l in range(i + 1, 8):
-                C[t, l] = C[t, l] - m * rows[l]
-            for s in range(t + 1, 16):
-                m = C[s, i] * ip
-                A[s] = A[s] - m * Rs
+                C[l] = C[l] - m * rows[i, l]
+            outer.append(jnp.where((lanes > j0 + i) & (lanes < j0 + 8), 0.0, Ri))
+        rs = lax.rsqrt(piv)
+        store(t, jnp.where(lanes < j0 + subs, R * rs, jnp.where(lanes == j0 + subs, rs, 0.0)))
+        for s in range(t + 1, 16):
+            D = [spread(A[s], j0 + i) for i in range(8)]
+            q = jnp.where(inside, 0.0, A[s])
+            for i in range(8):
+                q = q - D[i] * outer[i]
                 for l in range(i + 1, 8):
-                    C[s, l] = C[s, l] - m * rows[l]
-        rs = lax.rsqrt(piv)
-        inv = jnp.where(lanes < j0 + subs, R * rs, jnp.where(lanes == j0 + subs, rs, 0.0))
-        store(t, inv)
+                    D[l] = D[l] - D[i] * rows[i, l]
+            A[s] = q
 
 
 def split(x):
@@ -175,7 +182,7 @@
 BF16 = jnp.bfloat16
 
 def share_kernel(nx, n, x_ref, u_ref, v_ref, tab, xs, fs, sumx, rz, mine,
-                 own_s, xs_s, xs_r, rz_s, rz_r, aa_s, aa_r, ax_s, ax_r, bp_s, bp_r, bm_s, bm_r, tw_s, tw_r):
+                 own_s, xs_s, xs_r, rz_s, rz_r, aa_s, aa_r, ax_s, ax_r, bb_s, bb_r, tw_s, tw_r):
     row, col = lax.axis_index("row"), lax.axis_index("col")
     y, core = row // 2, row % 2
     x, z = col // n, col % n
@@ -277,26 +284,29 @@
     def pass_on(k, e):
         go(copy(piece(k, e), piece(k, e), tw_s.at[k, e], tw_r.at[k, e], twin))
 
-    def reach(e):
-        return (n // 2, n - 1 - n // 2) if e % 2 == 0 else (n - 1 - n // 2, n // 2)
-
     for e in range(nx):
         if e:
             copy(piece(0, e), piece(0, e), ax_s.at[e - 1], ax_r.at[e - 1], at_x(e)).wait_recv()
-        go(copy(piece(0, e), piece(0, e), bp_s.at[0, e], bp_r.at[0, e], at_b(1)))
-        go(copy(piece(0, e), piece(0, e), bm_s.at[0, e], bm_r.at[0, e], at_b(n - 1)))
+        for d in (1, n - 1, 2, n - 2):
+            go(copy(piece(0, e), piece(0, e), bb_s.at[d, e], bb_r.at[d, e], at_b(d)))
         pass_on(0, e)
-    for s in range(1, n // 2 + 1):
-        for e in range(nx):
-            plus, minus = reach(e)
-            for far, k, ss, rr, to in ((plus, s, bp_s, bp_r, 1), (minus, n - s, bm_s, bm_r, n - 1)):
-                if s > far:
-                    continue
-                ref = piece(k, e)
-                copy(ref, ref, ss.at[s - 1, e], rr.at[s - 1, e], at_b(to)).wait_recv()
-                if s < far:
-                    go(copy(ref, ref, ss.at[s, e], rr.at[s, e], at_b(to)))
-                pass_on(k, e)
+
+    def land(k, e):
+        copy(piece(k, e), piece(k, e), bb_s.at[k, e], bb_r.at[k, e], at_b(k)).wait_recv()
+
+    for e in range(nx):
+        for k, onward in ((2, (1, 2) if e % 2 == 0 else (1,)), (n - 2, (n - 1,) if e % 2 == 0 else (n - 1, n - 2))):
+            land(k, e)
+            for d in onward:
+                go(copy(piece(k, e), piece(k, e), bb_s.at[(k + d) % n, e], bb_r.at[(k + d) % n, e], at_b(d)))
+            pass_on(k, e)
+        for k in (1, n - 1):
+            land(k, e)
+            pass_on(k, e)
+    for e in range(nx):
+        for k in (3, n - 3, 4):
+            land(k, e)
+            pass_on(k, e)
     theirs = z * core + y * other
     for k in range(n):
         for e in range(nx):
@@ -312,7 +322,7 @@
     tab = (2, n, nx, n, block, 128)
     hbm = pl.BlockSpec(memory_space=pltpu.MemorySpace.HBM)
     pairs = []
-    for shape in ((nx - 1, 4), (n - 1,), (n - 1,), (nx - 1,), (n // 2, nx), (n // 2, nx), (n, nx)):
+    for shape in ((nx - 1, 4), (n - 1,), (n - 1,), (nx - 1,), (n, nx), (n, nx)):
         pairs += [dma(shape), dma(shape)]
     return pl.pallas_call(
         functools.partial(share_kernel, nx, n),

time: 81.7 us -> 73.9 us (0.905)
  Pallas kernels: 80.5 us -> 72.7 us
    pallas_call x1, Pallas kernels: 50 us -> 46 us  [share(): pl.pallas_call(functools.partial(share_kernel, nx, n), out_shape=jax.Shap...]
    pallas_call x1, Pallas kernels: 30.6 us -> 26.7 us  [f(): pl.pallas_call(functools.partial(kernel, rc), out_shape=jax.ShapeDtypeStr...]
where the time goes in v3:
time: 73.9 us; the launch traced here: 72.7 us
  Pallas kernels  72.7 us (98%)
    pallas_call x1, Pallas kernels, share(): pl.pallas_call(functools.partial(share_kernel, nx, n), out_shape=jax.Shap...  46 us
    pallas_call x1, Pallas kernels, f(): pl.pallas_call(functools.partial(kernel, rc), out_shape=jax.ShapeDtypeStr...  26.7 us

profile of v3, /device:TPU:1, one launch (start us, length us, event | category | flops | bytes accessed | tf_op | source)
XLA Modules:
  0.0 72.7 jit_solution(7895735271097093050)
XLA Ops:
  0.0 0.0 copy-start
  0.0 46.0 %shard_map.46.tab_ref = bf16[2,8,4,8,16,128]{5,4,3,2,1,0:T(8,128)(2,1)S(1)} custom-call(bf16[32,1024]{1,0:T(8,128)(2,1)} %bitcast.1, bf16[32,32]{1,0:T(8,128)(2,1)} %u_ref.1, bf16[32,32]{1,0:T(8,128)(2,1)} %v_ref.1), custom_call_target="tpu_custom_call" | custom-call | tf_op jit(solution)/shard_map/pallas_call | solution.py:327
  46.0 0.0 copy-done
  46.0 26.7 %shard_map.47 = f32[1024,512]{1,0:T(8,128)} custom-call(s32[16384]{0:T(1024)S(1)} %copy-done, bf16[2,8,4,8,16,128]{5,4,3,2,1,0:T(8,128)(2,1)S(1)} %shard_map.46.tab_ref), custom_call_target="tpu_custom_call" | custom-call | tf_op jit(solution)/shard_map/pallas_call | solution.py:161
Async XLA Ops:
  0.0 46.0 %copy-start = (s32[16384]{0:T(1024)S(1)}, s32[16384]{0:T(1024)}, u32[]{:S(2)}) copy-start(s32[16384]{0:T(1024)} %idx_ref.1) | copy-start | bytes 196612

commit v4 on v3

--- a/solution.py
+++ b/solution.py
@@ -20,7 +20,7 @@
     return jnp.broadcast_to(x[i : i + 1, :], (8, 128))
 
 
-def factor_block(load, store, lanes, subs):
+def factor_block(load, store, lanes, subs, hook):
     A = [load(t) for t in range(16)]
     for t in range(16):
         j0 = 8 * t
@@ -51,6 +51,7 @@
                 for l in range(i + 1, 8):
                     D[l] = D[l] - D[i] * rows[i, l]
             A[s] = q
+        hook(t)
 
 
 def split(x):
@@ -62,8 +63,18 @@
     return lax.dot_general(a, b, NT, preferred_element_type=F32)
 
 
-def kernel(rc, idx_ref, tab_ref, out_ref, t2, g32, gu, gv, sx, inv_ref, ch, cl):
+def three(a, b):
+    return dot(a[0], b[0]) + (dot(a[0], b[1]) + dot(a[1], b[0]))
+
+
+def kernel(rc, idx_hbm, tab_ref, out_hbm, out_ref, idx_ref, idx_sem, out_sem, t2, g32, gu, gv, sx, inv_ref, ch, cl, invh, invl, lh, ll):
     r, c = rc() if callable(rc) else rc
+    runs = [
+        pltpu.make_async_copy(idx_hbm.at[pl.ds(pl.multiple_of(first, 1024), 1024)], idx_ref.at[pl.ds(1024 * i, 1024)], idx_sem.at[i])
+        for i, first in enumerate((0, c // 2 * 1024, r * 1024))
+    ]
+    for run in runs:
+        run.start()
     lanes = lax.broadcasted_iota(jnp.int32, (8, 128), 1)
     subs = lax.broadcasted_iota(jnp.int32, (8, 128), 0)
 
@@ -88,9 +99,11 @@
             return 0
         lax.fori_loop(0, n // 16, body, 0)
 
+    for run in runs:
+        run.wait()
     pick(512, 0, 0)
-    pick(512, c * 512, 512)
-    pick(1024, r * 1024, 1024)
+    pick(512, 1024 + c % 2 * 512, 512)
+    pick(1024, 2048, 1024)
     wide = lax.broadcasted_iota(jnp.int32, (256, 128), 1)
 
     def masks(i, _):
@@ -103,57 +116,89 @@
     lax.fori_loop(0, 8, masks, 0)
 
     def gram(rows, cols):
-        a = lax.dot_general(gu[rows, :], gu[cols, :], NT, preferred_element_type=F32)
-        b = lax.dot_general(gv[rows, :], gv[cols, :], NT, preferred_element_type=F32)
-        return a * b
+        return dot(gu[rows, :], gu[cols, :]) * dot(gv[rows, :], gv[cols, :])
 
     il = lax.broadcasted_iota(jnp.int32, (256, 512), 0)
     ic = lax.broadcasted_iota(jnp.int32, (256, 512), 1)
-    for i in range(8):
+
+    def columns(i):
         rows = pl.ds(i * 256, 256)
         first = i * 256 if i < 2 else (c * 512 + (i - 2) * 256 if i < 4 else r * 1024 + (i - 4) * 256)
         sx[rows, :] = gram(rows, pl.ds(0, 512)) + jnp.where(il + first == ic, 1.0, 0.0)
+
+    def full(a, b):
+        return lax.dot_general(a, b, NT, precision=HI, preferred_element_type=F32)
+
+    def solve(k, rows):
+        cols = pl.ds(k * 128, 128)
+        b = three(split(sx[rows, cols]), (invh[k], invl[k]))
+        sx[rows, cols] = b
+        if k < 3:
+            rest = pl.ds(k * 128 + 128, 384 - k * 128)
+            sx[rows, rest] = sx[rows, rest] - three(split(b), (lh[rest, cols], ll[rest, cols]))
+
+    def block(i):
+        grow = il + (r * 1024 + i * 256)
+        return pl.ds(i * 256, 256), pl.ds(1024 + i * 256, 256), grow
+
+    def fill(i):
+        dst, rows, grow = block(i)
+        out_ref[dst, :] = gram(rows, pl.ds(512, 512)) + jnp.where(grow == ic + c * 512, 1.0, 0.0)
+
+    def product(rows, keep, cols):
+        return three(split(jnp.where(keep, sx[rows, cols], 0.0)), (ch[:, cols], cl[:, cols]))
+
+    def first_half(i):
+        dst, rows, grow = block(i)
+        out_ref[dst, :] = out_ref[dst, :] - product(rows, grow[:, :256] >= 256, pl.ds(0, 256))
+
+    def hook(k, t):
+        if k == 0:
+            if t < 6:
+                columns(2 + t)
+            elif t < 10:
+                fill(t - 6)
+        elif t < 12:
+            solve(k - 1, pl.ds(512 + 128 * t, 128))
+        elif k == 3:
+            if t == 12:
+                ch[:, :256], cl[:, :256] = split(sx[pl.ds(512, 512), pl.ds(0, 256)])
+            first_half(t - 12)
+
+    columns(0)
+    columns(1)
 
     for k in range(4):
         cols = pl.ds(k * 128, 128)
         factor_block(
             lambda t: sx[pl.ds(k * 128 + 8 * t, 8), cols],
-            lambda t, v: inv_ref.__setitem__((pl.ds(8 * t, 8), slice(None)), v),
-            lanes, subs,
+            lambda t, v: inv_ref.__setitem__((k, pl.ds(8 * t, 8), slice(None)), v),
+            lanes, subs, functools.partial(hook, k),
         )
-        for i in range(8):
-            rows = pl.ds(i * 256, 256)
-            if i * 256 + 256 <= k * 128:
-                continue
-            sx[rows, cols] = lax.dot_general(sx[rows, cols], inv_ref[...], NT, precision=HI, preferred_element_type=F32)
+        invh[k], invl[k] = split(inv_ref[k])
         if k < 3:
+            rows = pl.ds(k * 128, 512 - k * 128)
+            b = full(sx[rows, cols], inv_ref[k])
+            sx[rows, cols] = b
             rest = pl.ds(k * 128 + 128, 384 - k * 128)
-            for i in range(8):
-                if i * 256 + 256 <= k * 128 + 128:
-                    continue
-                rows = pl.ds(i * 256, 256)
-                sx[rows, rest] = sx[rows, rest] - lax.dot_general(
-                    sx[rows, cols], sx[rest, cols], NT, precision=HI, preferred_element_type=F32)
-
-    ch[...], cl[...] = split(sx[pl.ds(512, 512), :])
+            sx[rest, rest] = sx[rest, rest] - full(b[128:], b[128:])
+            lh[rest, cols], ll[rest, cols] = split(b[128:])
+    for i in range(6):
+        solve(3, pl.ds(512 + 256 * i, 256))
+    ch[:, 256:], cl[:, 256:] = split(sx[pl.ds(512, 512), pl.ds(256, 256)])
+
+    writes = []
     for i in range(4):
-        rows = pl.ds(1024 + i * 256, 256)
-        dst = pl.ds(i * 256, 256)
-        grow = il + (r * 1024 + i * 256)
-        s = gram(rows, pl.ds(512, 512)) + jnp.where(grow == ic + c * 512, 1.0, 0.0)
-        b = sx[rows, :]
-
-        @pl.when(c == 0)
-        def _():
-            lead = jnp.where(ic <= grow, b, jnp.where((grow < 256) & (ic >= 256), s, 0.0))
-            out_ref[dst, :] = jnp.where(grow < 512, lead, b)
-
-        @pl.when(c != 0)
-        def _():
-            keep = (grow >= 512) | ((grow >= 256) & (ic < 256))
-            bm = jnp.where(keep, b, 0.0)
-            bh, bl = split(bm)
-            out_ref[dst, :] = s - (dot(bh, ch[...]) + (dot(bh, cl[...]) + dot(bl, ch[...])))
+        dst, rows, grow = block(i)
+        s, b = out_ref[dst, :], sx[rows, :]
+        lead = jnp.where(ic <= grow, b, jnp.where((grow < 256) & (ic >= 256), s, 0.0))
+        panel = jnp.where(grow < 512, lead, b)
+        trailing = s - product(rows, grow[:, :256] >= 512, pl.ds(256, 256))
+        out_ref[dst, :] = jnp.where(c == 0, panel, trailing)
+        writes.append(pltpu.make_async_copy(out_ref.at[dst], out_hbm.at[dst], out_sem.at[i]))
+        writes[-1].start()
+    for write in writes:
+        write.wait()
 
 
 def local_part(rc):
@@ -161,15 +206,23 @@
         return pl.pallas_call(
             functools.partial(kernel, rc),
             out_shape=jax.ShapeDtypeStruct((1024, 512), F32),
-            in_specs=[pl.BlockSpec(memory_space=pltpu.SMEM), pl.BlockSpec(memory_space=pltpu.VMEM)],
-            out_specs=pl.BlockSpec(memory_space=pltpu.VMEM),
+            in_specs=[pl.BlockSpec(memory_space=pl.ANY), pl.BlockSpec(memory_space=pltpu.VMEM)],
+            out_specs=pl.BlockSpec(memory_space=pl.ANY),
             scratch_shapes=[
+                pltpu.VMEM((1024, 512), F32),
+                pltpu.SMEM((3072,), jnp.int32),
+                pltpu.SemaphoreType.DMA((3,)),
+                pltpu.SemaphoreType.DMA((4,)),
                 pltpu.VMEM((16384, 128), F32),
                 pltpu.VMEM((2048, 128), F32),
                 pltpu.VMEM((2048, 128), jnp.bfloat16),
                 pltpu.VMEM((2048, 128), jnp.bfloat16),
                 pltpu.VMEM((2048, 512), F32),
-                pltpu.VMEM((128, 128), F32),
+                pltpu.VMEM((4, 128, 128), F32),
+                pltpu.VMEM((512, 512), jnp.bfloat16),
+                pltpu.VMEM((512, 512), jnp.bfloat16),
+                pltpu.VMEM((4, 128, 128), jnp.bfloat16),
+                pltpu.VMEM((4, 128, 128), jnp.bfloat16),
                 pltpu.VMEM((512, 512), jnp.bfloat16),
                 pltpu.VMEM((512, 512), jnp.bfloat16),
             ],

time: 73.9 us -> 69.2 us (0.936); the launches traced: 72.7 us -> 69.1 us
  Pallas kernels: 72.7 us -> 68.9 us
    pallas_call x1, Pallas kernels: 26.7 us -> 22.9 us  [f(): pl.pallas_call(functools.partial(kernel, rc), out_shape=jax.ShapeDtypeStr...]
where the time goes in v4:
time: 69.2 us; the launch traced here: 69.1 us
  Pallas kernels  68.9 us (100%)
    pallas_call x1, Pallas kernels, share(): pl.pallas_call(functools.partial(share_kernel, nx, n), out_shape=jax.Shap...  46 us
    pallas_call x1, Pallas kernels, f(): pl.pallas_call(functools.partial(kernel, rc), out_shape=jax.ShapeDtypeStr...  22.9 us

profile of v4, /device:TPU:1, one launch (start us, length us, event | category | flops | bytes accessed | tf_op | source)
XLA Modules:
  0.0 69.1 jit_solution(5473558675267539574)
XLA Ops:
  0.0 0.0 copy-start
  0.0 46.0 %shard_map.46.tab_ref = bf16[2,8,4,8,16,128]{5,4,3,2,1,0:T(8,128)(2,1)S(1)} custom-call(bf16[32,1024]{1,0:T(8,128)(2,1)} %bitcast.1, bf16[32,32]{1,0:T(8,128)(2,1)} %u_ref.1, bf16[32,32]{1,0:T(8,128)(2,1)} %v_ref.1), custom_call_target="tpu_custom_call" | custom-call | tf_op jit(solution)/shard_map/pallas_call | solution.py:380
  46.0 0.0 copy-done
  46.0 22.9 %shard_map.47 = f32[1024,512]{1,0:T(8,128)} custom-call(s32[16384]{0:T(1024)S(1)} %copy-done, bf16[2,8,4,8,16,128]{5,4,3,2,1,0:T(8,128)(2,1)S(1)} %shard_map.46.tab_ref), custom_call_target="tpu_custom_call" | custom-call | tf_op jit(solution)/shard_map/pallas_call | solution.py:206
Async XLA Ops:
  0.0 46.0 %copy-start = (s32[16384]{0:T(1024)S(1)}, s32[16384]{0:T(1024)}, u32[]{:S(2)}) copy-start(s32[16384]{0:T(1024)} %idx_hbm.1) | copy-start | bytes 196612

commit v5 on v4

--- a/solution.py
+++ b/solution.py
@@ -340,7 +340,7 @@
     for e in range(nx):
         if e:
             copy(piece(0, e), piece(0, e), ax_s.at[e - 1], ax_r.at[e - 1], at_x(e)).wait_recv()
-        for d in (1, n - 1, 2, n - 2):
+        for d in (2, n - 2, 1, n - 1):
             go(copy(piece(0, e), piece(0, e), bb_s.at[d, e], bb_r.at[d, e], at_b(d)))
         pass_on(0, e)
 

time: 69.2 us -> 68.9 us (level)
  no operation moved by 1% of the time
where the time goes in v5:
time: 68.9 us; the launch traced here: 68.8 us
  Pallas kernels  68.6 us (100%)
    pallas_call x1, Pallas kernels, share(): pl.pallas_call(functools.partial(share_kernel, nx, n), out_shape=jax.Shap...  45.7 us
    pallas_call x1, Pallas kernels, f(): pl.pallas_call(functools.partial(kernel, rc), out_shape=jax.ShapeDtypeStr...  22.9 us

profile of v5, /device:TPU:1, one launch (start us, length us, event | category | flops | bytes accessed | tf_op | source)
XLA Modules:
  0.0 68.8 jit_solution(18123150029914627651)
XLA Ops:
  0.0 0.0 copy-start
  0.0 45.7 %shard_map.46.tab_ref = bf16[2,8,4,8,16,128]{5,4,3,2,1,0:T(8,128)(2,1)S(1)} custom-call(bf16[32,1024]{1,0:T(8,128)(2,1)} %bitcast.1, bf16[32,32]{1,0:T(8,128)(2,1)} %u_ref.1, bf16[32,32]{1,0:T(8,128)(2,1)} %v_ref.1), custom_call_target="tpu_custom_call" | custom-call | tf_op jit(solution)/shard_map/pallas_call | solution.py:380
  45.7 0.0 copy-done
  45.7 22.9 %shard_map.47 = f32[1024,512]{1,0:T(8,128)} custom-call(s32[16384]{0:T(1024)S(1)} %copy-done, bf16[2,8,4,8,16,128]{5,4,3,2,1,0:T(8,128)(2,1)S(1)} %shard_map.46.tab_ref), custom_call_target="tpu_custom_call" | custom-call | tf_op jit(solution)/shard_map/pallas_call | solution.py:206
Async XLA Ops:
  0.0 45.7 %copy-start = (s32[16384]{0:T(1024)S(1)}, s32[16384]{0:T(1024)}, u32[]{:S(2)}) copy-start(s32[16384]{0:T(1024)} %idx_hbm.1) | copy-start | bytes 196612
